TPU v7x, 128 devices: a whole 4x4x4 slice. The times are simulated.
128 devices in a mesh: leaf: 16 (over y_hi, x, core), rep: 8 (over y_lo, z).
Axes of the slice: x: 4, y: 4 (y_hi: 2, y_lo: 2; y = y_hi * 2 + y_lo), z: 4, core: 2. Of those that a mesh axis runs over, the one named last changes fastest.
Arguments:
- local_right: float32 [16, 8, 2048, 128], P('leaf', 'rep'), may hold values from -6 to 6
- local_inverse: bfloat16 [16, 8, 16, 128, 128], P('leaf', 'rep'), may hold values from -1 to 1.4, as said below
- local_below: bfloat16 [16, 8, 15, 128, 128], P('leaf', 'rep'), may hold values from -0.5 to 0.5
- local_parent: int32 [16, 8, 15], P('leaf', 'rep'), may hold values from 1 to 15, as said below
- local_coupling: bfloat16 [16, 8, 4, 384, 2048], P('leaf', 'rep'), may hold values from -0.1 to 0.1
- separator_right: float32 [15, 384, 128], replicated, may hold values from -6 to 6
- separator_inverse: bfloat16 [15, 3, 128, 128], replicated, may hold values from -1 to 1.4, as said below
- separator_lower: bfloat16 [15, 384, 384], replicated, may hold values from -0.3125 to 0.3125
- parent_coupling: bfloat16 [14, 384, 384], replicated, may hold values from -0.3125 to 0.3125
Outputs:
- local_solution: float32 [16, 8, 2048, 128], P('leaf', 'rep')
- separator_solution: float32 [16, 4, 384, 128], P('leaf')
Inputs may be any that keep to these rules, and one draw needn't show every extreme that they name: `local_parent`: entry k of a device's list is larger than k. `local_inverse`: every block is lower triangular. `separator_inverse`: every block is lower triangular.
All inputs are finite; a program needn't handle non-finite values.
Results may differ from a plain program's by a relative error of at most 0.035.
Values sent between devices are 32-bit elements; how exact they have to be, the bound alone decides.
No kernel may reach another device: no remote copies, remote signals or barrier semaphores. Data moves between devices by JAX's collectives and lax.ppermute only.
A program may use at most 128 MiB of HBM per device.

v0:
```python
import jax
import jax.numpy as jnp
from jax import lax
from jax.sharding import PartitionSpec as P

NB = 128
LB = 16
SB = 3


def swapped(value, axis, distance):
    mask = 2**distance
    pairs = [(source, source ^ mask) for source in range(lax.axis_size(axis))]
    return lax.ppermute(value, axis, pairs)


def apply_lower(matrix, vector):
    return jnp.dot(matrix, vector.astype(jnp.bfloat16), preferred_element_type=jnp.float32)


def apply_upper(matrix, vector):
    return jnp.dot(matrix.T, vector.astype(jnp.bfloat16), preferred_element_type=jnp.float32)


def right_lower(vector_rows, matrix):
    return jnp.dot(vector_rows.astype(jnp.bfloat16), matrix.T, preferred_element_type=jnp.float32)


def right_upper(vector_rows, matrix):
    return jnp.dot(vector_rows.astype(jnp.bfloat16), matrix, preferred_element_type=jnp.float32)


def block_lookup_tables(below, parents):
    targets = jnp.concatenate([parents, jnp.full((1,), LB, jnp.int32)])
    padded = jnp.concatenate([below, jnp.zeros((1, NB, NB), below.dtype)], axis=0)
    orders = jnp.arange(LB, dtype=jnp.int32)
    return (targets, padded, orders)


def local_forward(righthand, inverse, below, parents):
    columns = righthand.shape[1]
    blocks = righthand.reshape(LB, NB, columns)
    targets, padded, orders = block_lookup_tables(below, parents)

    def advance(carried, items):
        current, inv_block, low_block, target, number = items
        result = apply_lower(inv_block, current - carried[number])
        carried = carried.at[target].add(apply_lower(low_block, result))
        return (carried, result)

    start = jnp.zeros((LB + 1, NB, columns), jnp.float32)
    _, results = lax.scan(advance, start, (blocks, inverse, padded, targets, orders))
    return results.reshape(LB * NB, columns)


def local_backward(forward, update_terms, inverse, below, parents):
    columns = forward.shape[1]
    remains = (forward - update_terms).reshape(LB, NB, columns)
    targets, padded, orders = block_lookup_tables(below, parents)

    def retreat(carried, items):
        current, inv_block, low_block, target, number = items
        result = apply_upper(inv_block, current - apply_upper(low_block, carried[target]))
        carried = carried.at[number].set(result.astype(jnp.bfloat16))
        return (carried, result)

    start = jnp.zeros((LB + 1, NB, columns), jnp.bfloat16)
    _, results = lax.scan(retreat, start, (remains, inverse, padded, targets, orders), reverse=True)
    return results.reshape(LB * NB, columns)


def separator_forward(righthand, inverse, lowerpart):
    solved = []
    rounded = []
    for position in range(SB):
        current = righthand[:, position * NB : (position + 1) * NB]
        if position > 0:
            earlier = jnp.concatenate(rounded, axis=1)
            current = current - jnp.dot(
                earlier,
                lowerpart[position * NB : (position + 1) * NB, : position * NB].T,
                preferred_element_type=jnp.float32,
            )
        result = right_lower(current, inverse[position])
        solved.append(result)
        rounded.append(result.astype(jnp.bfloat16))
    return (jnp.concatenate(solved, axis=1), jnp.concatenate(rounded, axis=1))


def separator_backward(righthand, inverse, lowerpart):
    solved = [None] * SB
    rounded = [None] * SB
    for position in reversed(range(SB)):
        current = righthand[:, position * NB : (position + 1) * NB]
        if position < SB - 1:
            later = jnp.concatenate(rounded[position + 1 :], axis=1)
            current = current - right_upper(
                later, lowerpart[(position + 1) * NB :, position * NB : (position + 1) * NB]
            )
        result = right_upper(current, inverse[position])
        solved[position] = result
        rounded[position] = result.astype(jnp.bfloat16)
    return (jnp.concatenate(solved, axis=1), jnp.concatenate(rounded, axis=1))


def pick_entry(array, number):
    return lax.dynamic_index_in_dim(array, number, 0, keepdims=False)


def separator_chain(updates, separator_right, separator_inverse, separator_lower, parent_coupling):
    leaf_count = lax.axis_size("leaf")
    levels = leaf_count.bit_length() - 1
    leaf_index = lax.axis_index("leaf")
    remaining = updates
    forward_seps = []
    numbers = []
    inverse_blocks = []
    lowers = []
    for height in range(1, levels + 1):
        remaining = remaining + swapped(remaining, "leaf", height - 1)
        number = (leaf_count >> height) - 1 + (leaf_index >> height)
        right_rows = pick_entry(separator_right, number).T
        inverse = pick_entry(separator_inverse, number)
        lowerpart = pick_entry(separator_lower, number)
        result, result_round = separator_forward(right_rows - remaining[0], inverse, lowerpart)
        forward_seps.append(result)
        numbers.append(number)
        inverse_blocks.append(inverse)
        lowers.append(lowerpart)
        if height < levels:
            coupling_matrix = pick_entry(parent_coupling, number - 1)
            remaining = remaining[1:]
            remaining = remaining.at[0].add(
                jnp.dot(result_round, coupling_matrix.T, preferred_element_type=jnp.float32)
            )
    solutions = [None] * levels
    above_round = None
    for height in range(levels, 0, -1):
        upward = forward_seps[height - 1]
        if height < levels:
            coupling_matrix = pick_entry(parent_coupling, numbers[height - 1] - 1)
            upward = upward - right_upper(above_round, coupling_matrix)
        result, above_round = separator_backward(
            upward, inverse_blocks[height - 1], lowers[height - 1]
        )
        solutions[height - 1] = result
    return jnp.stack(solutions, axis=0)


def on_device(
    local_right,
    local_inverse,
    local_below,
    local_parent,
    local_coupling,
    separator_right,
    separator_inverse,
    separator_lower,
    parent_coupling,
):
    forward = local_forward(
        local_right[0, 0], local_inverse[0, 0], local_below[0, 0], local_parent[0, 0]
    )
    coupling_matrix = local_coupling[0, 0]
    forward_pass_rounded = forward.astype(jnp.bfloat16)
    partials = jnp.einsum(
        "ekx,xn->enk", coupling_matrix, forward_pass_rounded, preferred_element_type=jnp.float32
    )
    updates = lax.psum(partials, "rep")
    solved = separator_chain(
        updates, separator_right, separator_inverse, separator_lower, parent_coupling
    )
    rounded_solution_rows = solved.astype(jnp.bfloat16)
    update_terms = jnp.einsum(
        "apy,anp->yn", coupling_matrix, rounded_solution_rows, preferred_element_type=jnp.float32
    )
    local_solution = local_backward(
        forward, update_terms, local_inverse[0, 0], local_below[0, 0], local_parent[0, 0]
    )
    return (local_solution[None, None], jnp.swapaxes(solved, 1, 2)[None])


def solution(mesh):
    in_specs = (
        P("leaf", "rep", None, None),
        P("leaf", "rep", None, None, None),
        P("leaf", "rep", None, None, None),
        P("leaf", "rep", None),
        P("leaf", "rep", None, None, None),
        P(),
        P(),
        P(),
        P(),
    )
    out_specs = (P("leaf", "rep", None, None), P("leaf", None, None, None))
    return jax.shard_map(
        on_device, mesh=mesh, in_specs=in_specs, out_specs=out_specs, check_vma=False
    )
```

profile of v0, /device:TPU:0, one launch (start us, length us, event | category | flops | bytes accessed | tf_op | source)
XLA Modules:
  0.0 457.7 jit_solution(9730714361711297936)
XLA Ops:
  10.4 144.4 %while.33 = (s32[]{:T(128)}, f32[17,128,128]{2,1,0:T(8,128)}, f32[16,128,128]{2,1,0:T(8,128)S(1)}, s32[16]{0:T(128)S(1)}, bf16[16,128,128]{2,1,0:T(8,128)(2,1)S(...) while((s32[]{:T(128)}, f32[17,128,128]{2,1,0:T(8,128)}, ...), condition=%wide.region_2.3_spmd, body=%wide.region_0.2_spmd.sunk | while | flops 8470553 | bytes 462066 | solution.py:52
  17.2 2.2 fusion.409
  26.3 2.2 fusion.409
  35.3 2.2 fusion.409
  44.3 2.2 fusion.409
  53.4 2.2 fusion.409
  62.4 2.2 fusion.409
  71.4 2.2 fusion.409
  80.4 2.2 fusion.409
  89.5 2.2 fusion.409
  98.5 2.2 fusion.409
  107.5 2.2 fusion.409
  116.5 2.2 fusion.409
  125.5 2.2 fusion.409
  134.6 2.2 fusion.409
  143.6 2.2 fusion.409
  152.6 2.2 fusion.409
  154.9 6.0 %fusion.40 = f32[4,128,384]{2,1,0:T(8,128)} fusion(bf16[2048,128,1]{1,0,2:T(8,128)(2,1)S(1)} %bitcast.313, bf16[1,1,4,384,2048]{4,3,2,1,0:T(8,128)(2,1)} %param.27), kind=kOutput, calls=%fused_computation.38 | convolution fusion | flops 805306368 | bytes 7602176 | tf_op jit(solution)/shard_map/ekx,xn->enk/dot_general | solution.py:166
  161.0 78.8 %all-reduce.3.cloned.1.call-done = f32[4,128,384]{2,1,0:T(8,128)} async-done(((f32[4,128,384]{2,1,0:T(8,128)}), f32[4,128,384]{2,1,0:T(8,128)}) %all-reduce.3.cloned.1.call-update) | async-done | bytes 786448 | tf_op jit(solution)/shard_map/psum | solution.py:169
  239.8 2.0 constant_dynamic-slice_fusion.1
  242.6 2.4 dynamic-slice_bitcast_fusion
  250.4 1.9 fusion.332
  252.2 1.9 fusion.78
  256.5 13.8 %collective-permute-done.1 = f32[3,128,384]{2,1,0:T(8,128)} collective-permute-done((f32[3,128,384]{2,1,0:T(8,128)}, f32[3,128,384]{2,1,0:T(8,128)}, u32[]{:S(2)}, u32[]{:S(2)}) %collective-permute-start.1) | collective-permute-done | bytes 589856 | tf_op jit(solution)/shard_map/ppermute | solution.py:14
  274.9 1.9 fusion.341
  278.0 3.1 collective-permute-start.2
  282.8 7.6 %collective-permute-done.2 = f32[2,128,384]{2,1,0:T(8,128)} collective-permute-done((f32[2,128,384]{2,1,0:T(8,128)S(1)}, f32[2,128,384]{2,1,0:T(8,128)}, u32[]{:S(2)}, u32[]{:S(2)}) %collective-permute-start.2) | collective-permute-done | bytes 393248 | tf_op jit(solution)/shard_map/ppermute | solution.py:14
  296.7 1.9 slice_add_fusion
  298.6 2.7 collective-permute-start.3
  302.8 3.2 collective-permute-done.3
  321.9 3.8 fusion.37
  327.2 122.6 %while.34 = (s32[]{:T(128)}, bf16[17,128,128]{2,1,0:T(8,128)(2,1)S(1)}, f32[16,128,128]{2,1,0:T(8,128)S(1)}, s32[16]{0:T(128)S(1)}, bf16[16,128,128]{2,1,0:T(8,1...) while((s32[]{:T(128)}, ...), condition=%wide.region_6.7_spmd, body=%wide.region_4.6_spmd.sunk | while | flops 8454170 | bytes 363271 | solution.py:68
  (244 shorter events, 153.6 us)
Async XLA Ops:
  7.2 240.6 %copy-start = (bf16[15,3,128,128]{3,2,1,0:T(8,128)(2,1)S(1)}, bf16[15,3,128,128]{3,2,1,0:T(8,128)(2,1)}, u32[]{:S(2)}) copy-start(bf16[15,3,128,128]{3,2,1,0:T(8,128)(2,1)} %param.29) | copy-start | bytes 4423684
  7.2 232.6 %all-reduce.3.cloned.1.call-start = ((), (), s32[]{:S(2)}) async-start(), calls=%async_computation | async-start | bytes 1572864 | tf_op jit(solution)/shard_map/psum | solution.py:169
  7.2 3.2 copy-start.20
  154.8 6.1 %copy-start.2 = (bf16[16,128,128]{2,1,0:T(8,128)(2,1)}, bf16[16,128,128]{2,1,0:T(8,128)(2,1)S(1)}, u32[]{:S(2)}) copy-start(bf16[16,128,128]{2,1,0:T(8,128)(2,1)S(1)} %get-tuple-element.562) | copy-start | bytes 1572868
  239.8 5.2 %collective-permute-start = (f32[4,128,384]{2,1,0:T(8,128)}, f32[4,128,384]{2,1,0:T(8,128)}, u32[]{:S(2)}, u32[]{:S(2)}) collective-permute-start(f32[4,128,384]{2,1,0:T(8,128)} %all-reduce.3.cloned.1.call-done), channel_id=1, source_target_pairs={{0,8},{8,0},{16,24},{24,16},{32,40},{40,32},{48,56},{56,48},{64,72... | collective-permute-start | bytes 2359304 | tf_op jit(solution)/shard_map/ppermute | solution.py:14
  242.6 2.4 copy-start.10
  244.9 2.1 copy-start.6
  247.1 0.7 copy-start.8
  254.2 16.1 %collective-permute-start.1 = (f32[3,128,384]{2,1,0:T(8,128)}, f32[3,128,384]{2,1,0:T(8,128)}, u32[]{:S(2)}, u32[]{:S(2)}) collective-permute-start(f32[3,128,384]{2,1,0:T(8,128)} %fusion.78), channel_id=1, source_target_pairs={{0,16},{8,24},{16,0},{24,8},{32,48},{40,56},{48,32},{56,40},{64,80... | collective-permute-start | bytes 1769480 | tf_op jit(solution)/shard_map/ppermute | solution.py:14
  256.5 15.1 %copy-start.7 = (f32[1,384,128]{1,2,0:T(8,128)S(1)}, f32[1,384,128]{1,2,0:T(8,128)}, u32[]{:S(2)}) copy-start(f32[1,384,128]{1,2,0:T(8,128)} %copy.14) | copy-start | bytes 589828
  271.6 0.7 copy-start.9
  278.0 12.4 %collective-permute-start.2 = (f32[2,128,384]{2,1,0:T(8,128)S(1)}, f32[2,128,384]{2,1,0:T(8,128)}, u32[]{:S(2)}, u32[]{:S(2)}) collective-permute-start(f32[2,128,384]{2,1,0:T(8,128)S(1)} %fusion.76), channel_id=1, source_target_pairs={{0,32},{8,40},{16,48},{24,56},{32,0},{40,8},{48,16},{56,24},{64,96... | collective-permute-start | bytes 1179656 | tf_op jit(solution)/shard_map/ppermute | solution.py:14
  282.8 18.5 %copy-start.5 = (f32[1,384,128]{2,1,0:T(8,128)S(1)}, f32[1,384,128]{2,1,0:T(8,128)}, u32[]{:S(2)}) copy-start(f32[1,384,128]{2,1,0:T(8,128)} %get-tuple-element.317) | copy-start | bytes 589828
  298.6 7.4 %collective-permute-start.3 = (f32[1,128,384]{2,1,0:T(8,128)}, f32[1,128,384]{2,1,0:T(8,128)S(1)}, u32[]{:S(2)}, u32[]{:S(2)}) collective-permute-start(f32[1,128,384]{2,1,0:T(8,128)} %slice_add_fusion), channel_id=1, source_target_pairs={{0,64},{8,72},{16,80},{24,88},{32,96},{40,104},{48,112},{56,120},{... | collective-permute-start | bytes 589832 | tf_op jit(solution)/shard_map/ppermute | solution.py:14
  301.5 5.7 %copy-start.4 = (bf16[384,384]{1,0:T(8,128)(2,1)S(1)}, bf16[384,384]{1,0:T(8,128)(2,1)}, u32[]{:S(2)}) copy-start(bf16[384,384]{1,0:T(8,128)(2,1)} %get-tuple-element.310) | copy-start | bytes 884740
  302.8 6.0 %copy-start.15 = (f32[128,128]{0,1:T(8,128)S(1)}, f32[128,128]{0,1:T(8,128)}, u32[]{:S(2)}) copy-start(f32[128,128]{0,1:T(8,128)} %get-tuple-element.331) | copy-start | bytes 196612
  302.8 6.0 %copy-start.16 = (f32[128,128]{0,1:T(8,128)S(1)}, f32[128,128]{0,1:T(8,128)}, u32[]{:S(2)}) copy-start(f32[128,128]{0,1:T(8,128)} %get-tuple-element.335) | copy-start | bytes 196612
  302.8 6.0 %copy-start.19 = (f32[128,128]{0,1:T(8,128)S(1)}, f32[128,128]{0,1:T(8,128)}, u32[]{:S(2)}) copy-start(f32[128,128]{0,1:T(8,128)} %get-tuple-element.333) | copy-start | bytes 196612
  307.1 5.6 %copy-start.13 = (f32[128,128]{0,1:T(8,128)S(1)}, f32[128,128]{0,1:T(8,128)}, u32[]{:S(2)}) copy-start(f32[128,128]{0,1:T(8,128)} %get-tuple-element.325) | copy-start | bytes 196612
  307.1 5.6 %copy-start.14 = (f32[128,128]{0,1:T(8,128)S(1)}, f32[128,128]{0,1:T(8,128)}, u32[]{:S(2)}) copy-start(f32[128,128]{0,1:T(8,128)} %get-tuple-element.329) | copy-start | bytes 196612
  307.1 5.6 %copy-start.18 = (f32[128,128]{0,1:T(8,128)S(1)}, f32[128,128]{0,1:T(8,128)}, u32[]{:S(2)}) copy-start(f32[128,128]{0,1:T(8,128)} %get-tuple-element.327) | copy-start | bytes 196612
  308.8 7.8 %copy-start.11 = (f32[128,128]{0,1:T(8,128)S(1)}, f32[128,128]{0,1:T(8,128)}, u32[]{:S(2)}) copy-start(f32[128,128]{0,1:T(8,128)} %get-tuple-element.319) | copy-start | bytes 196612
  308.8 7.8 %copy-start.12 = (f32[128,128]{0,1:T(8,128)S(1)}, f32[128,128]{0,1:T(8,128)}, u32[]{:S(2)}) copy-start(f32[128,128]{0,1:T(8,128)} %get-tuple-element.323) | copy-start | bytes 196612
  308.8 7.8 %copy-start.17 = (f32[128,128]{0,1:T(8,128)S(1)}, f32[128,128]{0,1:T(8,128)}, u32[]{:S(2)}) copy-start(f32[128,128]{0,1:T(8,128)} %get-tuple-element.321) | copy-start | bytes 196612
  320.4 1.5 copy-start.1
  449.9 1.0 copy-start.3
Sparse Core Ops, SparseCore 0:
  161.1 78.6 all-reduce.2
where the time goes:
time: 463 us; the launch traced here: 458 us
  loops' own time  123 us (27%)
  matrix products  112 us (24%)
  waiting for transfers between devices  103 us (22%)
  local copies, waits for them, and re-layouts  55.8 us (12%)
  other arithmetic  41 us (9%)
  between operations  14.5 us (3%)
  starting transfers between devices  7.28 us (2%)
    psum x1, waiting for transfers between devices, on_device(): updates = lax.psum(partials, 'rep')  78.8 us
    another operation x1, loops' own time, local_forward(): lax.scan(advance, start, (blocks, inverse, padded, targets, orders))  62.2 us
    another operation x1, loops' own time, local_backward(): lax.scan(retreat, start, (remains, inverse, padded, targets, orders), rev...  61 us
    dot_general x32, matrix products, apply_lower(): jnp.dot(matrix, vector.astype(jnp.bfloat16), preferred_element_type=jnp.f...  51.9 us
    dynamic_slice x64, local copies, waits for them, and re-layouts, local_forward(): lax.scan(advance, start, (blocks, inverse, padded, targets, orders))  39 us
    ppermute x4, waiting for transfers between devices, swapped(): return lax.ppermute(value, axis, pairs)  24.6 us
    another operation x32, other arithmetic  23.2 us
    dot_general x16, matrix products, apply_upper(): jnp.dot(matrix.T, vector.astype(jnp.bfloat16), preferred_element_type=jnp...  19.2 us
  transfers between devices with their start and end apart: 5, of which 4 were waited for; matrix products, arithmetic and copies ran while one was open for 2% of the time, Pallas kernels for 0%

commit v1 on v0

--- a/solution.py
+++ b/solution.py
@@ -166,7 +166,8 @@
     partials = jnp.einsum(
         "ekx,xn->enk", coupling_matrix, forward_pass_rounded, preferred_element_type=jnp.float32
     )
-    updates = lax.psum(partials, "rep")
+    terms = lax.all_gather(partials, "rep")
+    updates = jnp.sum(terms, axis=0)
     solved = separator_chain(
         updates, separator_right, separator_inverse, separator_lower, parent_coupling
     )

time: 463 us -> 465 us (level)
    psum x1 -> x0, waiting for transfers between devices: 78.8 us -> none  [on_device(): updates = lax.psum(partials, 'rep')]
    all_gather x0 -> x1, waiting for transfers between devices: none -> 75.1 us  [on_device(): terms = lax.all_gather(partials, 'rep')]
where the time goes in v1:
time: 465 us; the launch traced here: 459 us
  loops' own time  123 us (26%)
  matrix products  112 us (24%)
  waiting for transfers between devices  99.2 us (21%)
  local copies, waits for them, and re-layouts  56.9 us (12%)
  other arithmetic  45.5 us (10%)
  between operations  14.5 us (3%)
  starting transfers between devices  7.46 us (2%)
    all_gather x1, waiting for transfers between devices, on_device(): terms = lax.all_gather(partials, 'rep')  75.1 us
    another operation x1, loops' own time, local_forward(): lax.scan(advance, start, (blocks, inverse, padded, targets, orders))  62.2 us
    another operation x1, loops' own time, local_backward(): lax.scan(retreat, start, (remains, inverse, padded, targets, orders), rev...  61 us
    dot_general x32, matrix products, apply_lower(): jnp.dot(matrix, vector.astype(jnp.bfloat16), preferred_element_type=jnp.f...  52.3 us
    dynamic_slice x64, local copies, waits for them, and re-layouts, local_forward(): lax.scan(advance, start, (blocks, inverse, padded, targets, orders))  39 us
    another operation x32, other arithmetic  24.2 us
    ppermute x4, waiting for transfers between devices, swapped(): return lax.ppermute(value, axis, pairs)  24.1 us
    dot_general x16, matrix products, apply_upper(): jnp.dot(matrix.T, vector.astype(jnp.bfloat16), preferred_element_type=jnp...  19.2 us
  transfers between devices with their start and end apart: 5, of which 4 were waited for; matrix products, arithmetic and copies ran while one was open for 2% of the time, Pallas kernels for 0%

profile of v1, /device:TPU:0, one launch (start us, length us, event | category | flops | bytes accessed | tf_op | source)
XLA Modules:
  0.0 459.1 jit_solution(243042955723787483)
XLA Ops:
  10.4 145.8 %while.33 = (s32[]{:T(128)}, f32[17,128,128]{2,1,0:T(8,128)}, f32[16,128,128]{2,1,0:T(8,128)S(1)}, s32[16]{0:T(128)S(1)}, bf16[16,128,128]{2,1,0:T(8,128)(2,1)S(...) while((s32[]{:T(128)}, f32[17,128,128]{2,1,0:T(8,128)}, ...), condition=%wide.region_2.3_spmd, body=%wide.region_0.2_spmd.sunk | while | flops 8470553 | bytes 462066 | solution.py:52
  17.3 2.2 fusion.409
  26.4 2.2 fusion.409
  35.5 2.2 fusion.409
  44.6 2.2 fusion.409
  53.7 2.2 fusion.409
  62.8 2.2 fusion.409
  71.9 2.2 fusion.409
  81.1 2.2 fusion.409
  90.2 2.2 fusion.409
  99.3 2.2 fusion.409
  108.4 2.2 fusion.409
  117.5 2.2 fusion.409
  126.6 2.2 fusion.409
  135.7 2.2 fusion.409
  144.9 2.2 fusion.409
  154.0 2.2 fusion.409
  156.3 6.0 %fusion.40 = f32[4,128,384]{2,1,0:T(8,128)} fusion(bf16[2048,128,1]{1,0,2:T(8,128)(2,1)S(1)} %bitcast.315, bf16[1,1,4,384,2048]{4,3,2,1,0:T(8,128)(2,1)} %param.27), kind=kOutput, calls=%fused_computation.38 | convolution fusion | flops 805306368 | bytes 7602176 | tf_op jit(solution)/shard_map/ekx,xn->enk/dot_general | solution.py:166
  162.4 75.1 %all-gather.3.cloned.1.call-done = f32[32,128,384]{2,1,0:T(8,128)} async-done(((f32[4,128,384]{2,1,0:T(8,128)}), f32[32,128,384]{2,1,0:T(8,128)}) %all-gather.3.cloned.1.call-update) | async-done | bytes 6291472 | tf_op jit(solution)/shard_map/all_gather | solution.py:169
  237.4 3.2 reduce_sum.9
  240.8 2.2 constant_dynamic-slice_fusion.1
  244.7 2.3 dynamic-slice_bitcast_fusion
  252.7 1.9 fusion.332
  254.6 1.9 fusion.78
  258.8 13.6 %collective-permute-done.1 = f32[3,128,384]{2,1,0:T(8,128)} collective-permute-done((f32[3,128,384]{2,1,0:T(8,128)}, f32[3,128,384]{2,1,0:T(8,128)}, u32[]{:S(2)}, u32[]{:S(2)}) %collective-permute-start.1) | collective-permute-done | bytes 589856 | tf_op jit(solution)/shard_map/ppermute | solution.py:14
  277.1 1.9 fusion.341
  280.2 3.1 collective-permute-start.2
  285.0 7.4 %collective-permute-done.2 = f32[2,128,384]{2,1,0:T(8,128)} collective-permute-done((f32[2,128,384]{2,1,0:T(8,128)S(1)}, f32[2,128,384]{2,1,0:T(8,128)}, u32[]{:S(2)}, u32[]{:S(2)}) %collective-permute-start.2) | collective-permute-done | bytes 393248 | tf_op jit(solution)/shard_map/ppermute | solution.py:14
  300.0 2.8 collective-permute-start.3
  304.3 3.1 collective-permute-done.3
  323.2 3.8 fusion.37
  328.6 122.6 %while.34 = (s32[]{:T(128)}, bf16[17,128,128]{2,1,0:T(8,128)(2,1)S(1)}, f32[16,128,128]{2,1,0:T(8,128)S(1)}, s32[16]{0:T(128)S(1)}, bf16[16,128,128]{2,1,0:T(8,1...) while((s32[]{:T(128)}, ...), condition=%wide.region_6.7_spmd, body=%wide.region_4.6_spmd.sunk | while | flops 8454170 | bytes 363271 | solution.py:68
  (247 shorter events, 157.2 us)
Async XLA Ops:
  7.2 242.9 %copy-start = (bf16[15,3,128,128]{3,2,1,0:T(8,128)(2,1)S(1)}, bf16[15,3,128,128]{3,2,1,0:T(8,128)(2,1)}, u32[]{:S(2)}) copy-start(bf16[15,3,128,128]{3,2,1,0:T(8,128)(2,1)} %param.29) | copy-start | bytes 4423684
  7.2 230.3 %all-gather.3.cloned.1.call-start = ((), (), s32[]{:S(2)}) async-start(), calls=%async_computation | async-start | bytes 7077888 | tf_op jit(solution)/shard_map/all_gather | solution.py:169
  7.2 3.2 copy-start.21
  156.2 6.1 %copy-start.3 = (bf16[16,128,128]{2,1,0:T(8,128)(2,1)}, bf16[16,128,128]{2,1,0:T(8,128)(2,1)S(1)}, u32[]{:S(2)}) copy-start(bf16[16,128,128]{2,1,0:T(8,128)(2,1)S(1)} %get-tuple-element.572) | copy-start | bytes 1572868
  240.6 6.4 %copy-start.2 = (f32[4,128,384]{2,1,0:T(8,128)}, f32[4,128,384]{2,1,0:T(8,128)S(1)}, u32[]{:S(2)}) copy-start(f32[4,128,384]{2,1,0:T(8,128)S(1)} %reduce_sum.9) | copy-start | bytes 2359300
  240.6 6.3 %collective-permute-start = (f32[4,128,384]{2,1,0:T(8,128)S(1)}, f32[4,128,384]{2,1,0:T(8,128)}, u32[]{:S(2)}, u32[]{:S(2)}) collective-permute-start(f32[4,128,384]{2,1,0:T(8,128)S(1)} %reduce_sum.9), channel_id=1, source_target_pairs={{0,8},{8,0},{16,24},{24,16},{32,40},{40,32},{48,56},{56,48},{64,72... | collective-permute-start | bytes 2359304 | tf_op jit(solution)/shard_map/ppermute | solution.py:14
  247.0 2.4 copy-start.7
  249.4 0.7 copy-start.9
  256.5 15.9 %collective-permute-start.1 = (f32[3,128,384]{2,1,0:T(8,128)}, f32[3,128,384]{2,1,0:T(8,128)}, u32[]{:S(2)}, u32[]{:S(2)}) collective-permute-start(f32[3,128,384]{2,1,0:T(8,128)} %fusion.78), channel_id=1, source_target_pairs={{0,16},{8,24},{16,0},{24,8},{32,48},{40,56},{48,32},{56,40},{64,80... | collective-permute-start | bytes 1769480 | tf_op jit(solution)/shard_map/ppermute | solution.py:14
  258.8 14.9 %copy-start.8 = (f32[1,384,128]{1,2,0:T(8,128)S(1)}, f32[1,384,128]{1,2,0:T(8,128)}, u32[]{:S(2)}) copy-start(f32[1,384,128]{1,2,0:T(8,128)} %copy.25) | copy-start | bytes 589828
  273.8 0.7 copy-start.10
  280.2 12.2 %collective-permute-start.2 = (f32[2,128,384]{2,1,0:T(8,128)S(1)}, f32[2,128,384]{2,1,0:T(8,128)}, u32[]{:S(2)}, u32[]{:S(2)}) collective-permute-start(f32[2,128,384]{2,1,0:T(8,128)S(1)} %fusion.76), channel_id=1, source_target_pairs={{0,32},{8,40},{16,48},{24,56},{32,0},{40,8},{48,16},{56,24},{64,96... | collective-permute-start | bytes 1179656 | tf_op jit(solution)/shard_map/ppermute | solution.py:14
  285.0 17.8 %copy-start.6 = (f32[1,384,128]{2,1,0:T(8,128)S(1)}, f32[1,384,128]{2,1,0:T(8,128)}, u32[]{:S(2)}) copy-start(f32[1,384,128]{2,1,0:T(8,128)} %get-tuple-element.325) | copy-start | bytes 589828
  296.9 1.8 copy-start.11
  300.0 7.4 %collective-permute-start.3 = (f32[1,128,384]{2,1,0:T(8,128)S(1)}, f32[1,128,384]{2,1,0:T(8,128)}, u32[]{:S(2)}, u32[]{:S(2)}) collective-permute-start(f32[1,128,384]{2,1,0:T(8,128)S(1)} %slice_add_fusion), channel_id=1, source_target_pairs={{0,64},{8,72},{16,80},{24,88},{32,96},{40,104},{48,112},{56,120},{... | collective-permute-start | bytes 589832 | tf_op jit(solution)/shard_map/ppermute | solution.py:14
  302.9 5.6 %copy-start.5 = (bf16[384,384]{1,0:T(8,128)(2,1)S(1)}, bf16[384,384]{1,0:T(8,128)(2,1)}, u32[]{:S(2)}) copy-start(bf16[384,384]{1,0:T(8,128)(2,1)} %get-tuple-element.318) | copy-start | bytes 884740
  304.3 5.8 %copy-start.16 = (f32[128,128]{0,1:T(8,128)S(1)}, f32[128,128]{0,1:T(8,128)}, u32[]{:S(2)}) copy-start(f32[128,128]{0,1:T(8,128)} %get-tuple-element.339) | copy-start | bytes 196612
  304.3 5.8 %copy-start.17 = (f32[128,128]{0,1:T(8,128)S(1)}, f32[128,128]{0,1:T(8,128)}, u32[]{:S(2)}) copy-start(f32[128,128]{0,1:T(8,128)} %get-tuple-element.343) | copy-start | bytes 196612
  304.3 5.9 %copy-start.20 = (f32[128,128]{0,1:T(8,128)S(1)}, f32[128,128]{0,1:T(8,128)}, u32[]{:S(2)}) copy-start(f32[128,128]{0,1:T(8,128)} %get-tuple-element.341) | copy-start | bytes 196612
  308.5 5.6 %copy-start.14 = (f32[128,128]{0,1:T(8,128)S(1)}, f32[128,128]{0,1:T(8,128)}, u32[]{:S(2)}) copy-start(f32[128,128]{0,1:T(8,128)} %get-tuple-element.333) | copy-start | bytes 196612
  308.5 5.6 %copy-start.15 = (f32[128,128]{0,1:T(8,128)S(1)}, f32[128,128]{0,1:T(8,128)}, u32[]{:S(2)}) copy-start(f32[128,128]{0,1:T(8,128)} %get-tuple-element.337) | copy-start | bytes 196612
  308.5 5.6 %copy-start.19 = (f32[128,128]{0,1:T(8,128)S(1)}, f32[128,128]{0,1:T(8,128)}, u32[]{:S(2)}) copy-start(f32[128,128]{0,1:T(8,128)} %get-tuple-element.335) | copy-start | bytes 196612
  310.1 7.8 %copy-start.12 = (f32[128,128]{0,1:T(8,128)S(1)}, f32[128,128]{0,1:T(8,128)}, u32[]{:S(2)}) copy-start(f32[128,128]{0,1:T(8,128)} %get-tuple-element.327) | copy-start | bytes 196612
  310.1 7.8 %copy-start.13 = (f32[128,128]{0,1:T(8,128)S(1)}, f32[128,128]{0,1:T(8,128)}, u32[]{:S(2)}) copy-start(f32[128,128]{0,1:T(8,128)} %get-tuple-element.331) | copy-start | bytes 196612
  310.1 7.8 %copy-start.18 = (f32[128,128]{0,1:T(8,128)S(1)}, f32[128,128]{0,1:T(8,128)}, u32[]{:S(2)}) copy-start(f32[128,128]{0,1:T(8,128)} %get-tuple-element.329) | copy-start | bytes 196612
  321.7 1.5 copy-start.1
  451.2 1.0 copy-start.4
Sparse Core Ops, SparseCore 0:
  162.5 74.9 all-gather.2
